TPU v7x, 256 devices: a whole 4x4x8 slice. The times are simulated.
256 devices in a mesh: strike: 64 (over y, z, core), dip: 4 (over x).
Axes of the slice: x: 4, y: 4, z: 8, core: 2. Of those that a mesh axis runs over, the one named last changes fastest.
Arguments:
- slip_rate: float32 [3, 4096, 1024], P(None, 'strike', 'dip'), may hold values from -6 to 6
- history: bfloat16 [4, 3, 2, 1024, 4096], P(None, None, None, ('strike', 'dip')), may hold values from -6 to 6
- lengths: int32 [1024, 4096], P(('strike', 'dip')), may hold values from 1 to 4, as said below
- prestress: float32 [2, 4096, 1024], P(None, 'strike', 'dip'), may hold values from -8 to 8
- normal_stress: float32 [4096, 1024], P('strike', 'dip'), may hold values from 8 to 16
- direct_effect: float32 [4096, 1024], P('strike', 'dip'), may hold values from 0.01 to 0.04
- state_log: float32 [4096, 1024], P('strike', 'dip'), may hold values from 1 to 5
Outputs:
- next_rates: float32 [3, 4096, 1024], P(None, 'strike', 'dip')
- next_state: float32 [4096, 1024], P('strike', 'dip')
Inputs may be any that keep to these rules, and one draw needn't show every extreme that they name: `lengths`: how many of the newest slip-rate spectra enter each wavenumber's stress transfer.
All inputs are finite; a program needn't handle non-finite values.
Results may differ from a plain program's by a relative error of at most 0.0003.
Values sent between devices are 32-bit elements; how exact they have to be, the bound alone decides.
No kernel may reach another device: no remote copies, remote signals or barrier semaphores. Data moves between devices by JAX's collectives and lax.ppermute only.
A program may use at most 128 MiB of HBM per device.

v0:
```python
import math
import jax
import jax.numpy as jnp
from jax import lax
from jax.sharding import PartitionSpec as P

HIST = 4
NEWTON = 2
time_step = 0.5
coupling = 0.5
decay_rate = 0.05
shear_speed = 0.6
opening_speed = 1.7
radiation = 0.5
healing = 1.0
slip_length = 2.0
highest = lax.Precision.HIGHEST


def area_sine(ratio):
    return jnp.log(ratio + jnp.sqrt(ratio * ratio + 1.0))


def wave_geometry(dip_modes, strike_modes, dip_cells, strike_cells):
    signed_dip = jnp.where(2 * dip_modes < dip_cells, dip_modes, dip_modes - dip_cells)
    signed_strike = jnp.where(
        2 * strike_modes < strike_cells, strike_modes, strike_modes - strike_cells
    )
    wave_dip = signed_dip.astype(jnp.float32) * (2.0 * math.pi / dip_cells)
    wave_strike = signed_strike.astype(jnp.float32) * (2.0 * math.pi / strike_cells)
    modulus = jnp.sqrt(wave_strike * wave_strike + wave_dip * wave_dip)
    anchor = (signed_dip == 0) & (signed_strike == 0)
    safe_modulus = jnp.where(anchor, 1.0, modulus)
    unit_strike = jnp.where(anchor, 1.0, wave_strike / safe_modulus)
    unit_dip = jnp.where(anchor, 0.0, wave_dip / safe_modulus)
    return (modulus, unit_strike, unit_dip)


def delay_mixing(geometry, delay):
    modulus, unit_strike, unit_dip = geometry
    phase_arg = modulus * (time_step * (delay + 1.0))
    envelope = -coupling * time_step * modulus * jnp.exp(-decay_rate * phase_arg)
    mode_two = envelope * jnp.cos(phase_arg)
    mode_three = envelope * jnp.cos(shear_speed * phase_arg)
    mode_one = envelope * jnp.cos(opening_speed * phase_arg)
    mix_along = unit_strike * unit_strike * mode_two + unit_dip * unit_dip * mode_three
    mix_cross = unit_strike * unit_dip * (mode_two - mode_three)
    mix_across = unit_dip * unit_dip * mode_two + unit_strike * unit_strike * mode_three
    return (mix_along, mix_cross, mix_across, mode_one)


def delay_term(spectrum, mixing, active):
    mix_along, mix_cross, mix_across, mode_one = mixing
    force_strike = (mix_along * spectrum[0] + mix_cross * spectrum[1]) * active
    force_dip = (mix_cross * spectrum[0] + mix_across * spectrum[1]) * active
    force_open = mode_one * spectrum[2] * active
    return jnp.stack([force_strike, force_dip, force_open])


def friction_step(force_field, prestress, normal_stress, direct_effect, state_log):
    load_strike = prestress[0] + force_field[0]
    load_dip = prestress[1] + force_field[1]
    traction = jnp.sqrt(load_strike * load_strike + load_dip * load_dip)
    strength = direct_effect * normal_stress
    factor = 2.0 * radiation * jnp.exp(-state_log)
    estimate = jnp.minimum(traction / strength, area_sine(traction / factor))
    for repeat in range(NEWTON):
        residual = traction - strength * estimate - factor * jnp.sinh(estimate)
        estimate = estimate + residual / (strength + factor * jnp.cosh(estimate))
    slip_speed = (traction - strength * estimate) / radiation
    unit_scale = slip_speed / jnp.maximum(traction, 1.0)
    new_rates = jnp.stack(
        [unit_scale * load_strike, unit_scale * load_dip, force_field[2] / radiation]
    )
    new_state = state_log + time_step * (healing * jnp.exp(-state_log) - slip_speed / slip_length)
    return (new_rates, new_state)


def phase_table(first_index, second_index, period):
    turn_count = first_index[:, None] * second_index[None, :] % period
    angle_table = turn_count.astype(jnp.float32) * (2.0 * math.pi / period)
    return (jnp.cos(angle_table), jnp.sin(angle_table))


def contract(pattern, first_operand, second_operand):
    return jnp.einsum(pattern, first_operand, second_operand, precision=highest)


def pair_section(part_real, part_imag, pattern, cos_table, sin_table, sign):
    out_real = contract(pattern, part_real, cos_table) - sign * contract(
        pattern, part_imag, sin_table
    )
    out_imag = contract(pattern, part_imag, cos_table) + sign * contract(
        pattern, part_real, sin_table
    )
    return (out_real, out_imag)


def twist_phase(part_real, part_imag, cos_table, sin_table, sign):
    out_real = cos_table * part_real - sign * sin_table * part_imag
    out_imag = cos_table * part_imag + sign * sin_table * part_real
    return (out_real, out_imag)


def shards(slip_rate, history, lengths, prestress, normal_stress, direct_effect, state_log):
    strike_count = lax.axis_size("strike")
    dip_count = lax.axis_size("dip")
    strike_index = lax.axis_index("strike")
    dip_index = lax.axis_index("dip")
    row_count = slip_rate.shape[1]
    dip_block = slip_rate.shape[2]
    mode_rows = history.shape[3]
    strike_cells = history.shape[4]
    dip_cells = dip_block * dip_count
    unit_modes = dip_count * mode_rows
    norm_dip = 1.0 / math.sqrt(dip_cells)
    norm_strike = 1.0 / math.sqrt(strike_cells)
    local_modes = jnp.arange(mode_rows, dtype=jnp.int32)
    dip_modes = (strike_index * dip_count + dip_index) * mode_rows + local_modes
    strike_modes = jnp.arange(strike_cells, dtype=jnp.int32)
    geometry = wave_geometry(dip_modes[:, None], strike_modes[None, :], dip_cells, strike_cells)
    coarse_all = jnp.arange(unit_modes, dtype=jnp.int32)
    coarse_own = dip_index * mode_rows + local_modes
    outer_index = jnp.arange(strike_count, dtype=jnp.int32)
    inner_index = jnp.arange(row_count, dtype=jnp.int32)
    cos_outer, sin_outer = phase_table(outer_index, outer_index, strike_count)
    cos_bend, sin_bend = phase_table(outer_index, inner_index, strike_cells)
    cos_bend = cos_bend * norm_strike
    sin_bend = sin_bend * norm_strike
    cos_inner, sin_inner = phase_table(inner_index, inner_index, row_count)

    def strike_forward(spectral):
        item_count = spectral.shape[0]
        grid_view = spectral.reshape(item_count, 2, mode_rows, strike_count, row_count)
        section_real, section_imag = pair_section(
            grid_view[:, 0], grid_view[:, 1], "ngpr,kp->ngkr", cos_outer, sin_outer, -1.0
        )
        bent_real, bent_imag = twist_phase(section_real, section_imag, cos_bend, sin_bend, -1.0)
        out_real, out_imag = pair_section(
            bent_real, bent_imag, "ngkr,rm->ngmk", cos_inner, sin_inner, -1.0
        )
        return jnp.stack([out_real, out_imag], axis=1).reshape(
            item_count, 2, mode_rows, strike_cells
        )

    def strike_inverse(spectral):
        grid_view = spectral.reshape(3, 2, mode_rows, row_count, strike_count)
        section_real, section_imag = pair_section(
            grid_view[:, 0], grid_view[:, 1], "ngmk,rm->ngrk", cos_inner, sin_inner, 1.0
        )
        bent_real, bent_imag = twist_phase(section_real, section_imag, cos_bend.T, sin_bend.T, 1.0)
        out_real, out_imag = pair_section(
            bent_real, bent_imag, "ngrk,kp->ngpr", cos_outer, sin_outer, 1.0
        )
        return jnp.stack([out_real, out_imag], axis=1).reshape(3, 2, mode_rows, strike_cells)

    def to_modes(space_field):
        gathered = lax.all_gather(space_field, "dip", axis=2, tiled=True)
        cos_first, sin_first = phase_table(coarse_all, coarse_own, unit_modes)
        cos_twist, sin_twist = phase_table(outer_index, coarse_own, dip_cells)
        grid_view = gathered.reshape(3, row_count, unit_modes, strike_count)
        first_real = contract("cxab,au->cxbu", grid_view, cos_first)
        first_imag = -contract("cxab,au->cxbu", grid_view, sin_first)
        bent_real, bent_imag = twist_phase(
            first_real, first_imag, cos_twist * norm_dip, sin_twist * norm_dip, -1.0
        )
        out_real, out_imag = pair_section(
            bent_real, bent_imag, "cxbi,bs->csix", cos_outer, sin_outer, -1.0
        )
        dip_spec = jnp.stack([out_real, out_imag], axis=1).reshape(3, 2, dip_block, row_count)
        return strike_forward(
            lax.all_to_all(dip_spec, "strike", split_axis=2, concat_axis=3, tiled=True)
        )

    def to_space(mode_field):
        mixed_rows = strike_inverse(mode_field)
        dip_spec = lax.all_to_all(mixed_rows, "strike", split_axis=3, concat_axis=2, tiled=True)
        gathered = lax.all_gather(dip_spec, "dip", axis=2, tiled=True)
        grid_view = gathered.reshape(3, 2, dip_count, strike_count, mode_rows, row_count)
        cos_last, sin_last = phase_table(coarse_own, coarse_all, unit_modes)
        first_real, first_imag = pair_section(
            grid_view[:, 0], grid_view[:, 1], "cdsix,bs->cxbdi", cos_outer, sin_outer, 1.0
        )
        first_real = first_real.reshape(3, row_count, strike_count, unit_modes)
        first_imag = first_imag.reshape(3, row_count, strike_count, unit_modes)
        cos_twist, sin_twist = phase_table(outer_index, coarse_all, dip_cells)
        bent_real, bent_imag = twist_phase(
            first_real, first_imag, cos_twist * norm_dip, sin_twist * norm_dip, 1.0
        )
        space_part = contract("cxbu,au->cxab", bent_real, cos_last) - contract(
            "cxbu,au->cxab", bent_imag, sin_last
        )
        return space_part.reshape(3, row_count, dip_block)

    def transfer(recent):
        recent_count = len(recent)
        summed = jnp.zeros(recent[0].shape, jnp.float32)
        for offset in range(HIST):
            if offset < recent_count:
                source = recent[offset]
            else:
                source = history[offset - recent_count].astype(jnp.float32)
            active = (offset < lengths).astype(jnp.float32)
            summed = summed + delay_term(source, delay_mixing(geometry, float(offset)), active)
        return summed

    first_spec = to_modes(slip_rate)
    force_field = to_space(transfer([first_spec]))
    next_rates, next_state = friction_step(
        force_field, prestress, normal_stress, direct_effect, state_log
    )
    second_spec = to_modes(next_rates)
    force_field = to_space(transfer([second_spec, first_spec]))
    next_rates, next_state = friction_step(
        force_field, prestress, normal_stress, direct_effect, next_state
    )
    return (next_rates, next_state)


def solution(mesh):
    return jax.shard_map(
        shards,
        mesh=mesh,
        in_specs=(
            P(None, "strike", "dip"),
            P(None, None, None, ("strike", "dip"), None),
            P(("strike", "dip"), None),
            P(None, "strike", "dip"),
            P("strike", "dip"),
            P("strike", "dip"),
            P("strike", "dip"),
        ),
        out_specs=(P(None, "strike", "dip"), P("strike", "dip")),
        check_vma=False,
    )
```

profile of v0, /device:TPU:1, one launch (start us, length us, event | category | flops | bytes accessed | tf_op | source)
XLA Modules:
  0.0 520.3 jit_solution(6019969516380714102)
XLA Ops:
  7.3 13.1 %all_gather.12 = f32[3,64,1024]{2,1,0:T(8,128)S(1)} all-gather(f32[3,64,256]{2,1,0:T(8,128)} %param.7), channel_id=1, replica_groups=mesh['strike'=64,'dip'=4] {'dip'}, dimensions={2}, use_global_device_ids=true | all-gather | bytes 983040 | tf_op jit(solution)/shard_map/all_gather | solution.py:158
  29.6 1.6 reshape.1792
  31.2 13.9 %all-to-all-start = ((f32[64,1,1536]{2,1,0:T(1,128)}), f32[64,1,1536]{2,1,0:T(1,128)S(1)}, u32[]{:S(2)}, u32[]{:S(2)}) async-start(f32[64,1,1536]{2,1,0:T(1,128)} %reshape.1792), calls=%async_computation | async-start | bytes 786432 | tf_op jit(solution)/shard_map/all_to_all | solution.py:172
  45.9 4.1 multiply_add_fusion.20
  60.7 2.8 multiply_add_fusion.5
  64.2 1.6 reduce
  84.6 10.5 %copy.366 = f32[3,1,4,4096]{2,1,0,3:T(1,128)} copy(f32[3,1,4,4096]{3,2,0,1:T(4,128)S(1)} %stack.171) | data formatting | bytes 393216 | tf_op jit(solution)/shard_map/stack | solution.py:155
  96.7 10.3 %copy.367 = f32[3,1,4,4096]{2,1,0,3:T(1,128)} copy(f32[3,1,4,4096]{3,2,0,1:T(4,128)S(1)} %stack.172) | data formatting | bytes 393216 | tf_op jit(solution)/shard_map/stack | solution.py:155
  107.0 16.7 %fusion.506 = f32[4096,3,2,4]{3,2,1,0:T(2,128)} fusion(f32[3,1,4,4096]{2,1,0,3:T(1,128)} %copy.367, f32[3,1,4,4096]{2,1,0,3:T(1,128)} %copy.366), kind=kLoop, calls=%fused_computation.664 | loop fusion | flops 98304 | bytes 786432
  123.7 16.7 %reshape.1794 = f32[64,1,1536]{2,1,0:T(1,128)S(1)} reshape(f32[4096,3,2,4]{3,2,1,0:T(2,128)} %fusion.506) | data formatting | bytes 786432
  140.4 24.7 %all_to_all.66 = f32[64,1,1536]{2,1,0:T(1,128)S(1)} all-to-all(f32[64,1,1536]{2,1,0:T(1,128)S(1)} %reshape.1794), channel_id=1, replica_groups=mesh['strike'=64,'dip'=4] {'strike'}, dimensions={0} | all-to-all | bytes 786432 | tf_op jit(solution)/shard_map/all_to_all | solution.py:177
  165.1 1.6 reduce.1
  166.7 21.1 %reshape.1795 = f32[4096,3,2,4]{3,2,1,0:T(2,128)} reshape(f32[64,1536]{1,0:T(8,128)S(1)} %reduce.1) | data formatting | bytes 786432
  187.8 16.1 %copy.455 = f32[3,2,4,64,64]{4,3,2,1,0:T(8,128)S(1)} copy(f32[3,2,4,64,64]{2,1,0,4,3:T(2,128)} %bitcast.476) | data formatting | bytes 786432 | tf_op jit(solution)/shard_map/all_to_all | solution.py:177
  204.0 1.4 copy.369
  205.5 38.9 %all-gather.3.cloned.1.call-done = f32[3,2,1024,64]{3,2,1,0:T(8,128)} async-done(((f32[3,2,256,64]{3,2,1,0:T(8,128)}), f32[3,2,1024,64]{3,2,1,0:T(8,128)}) %all-gather.3.cloned.1.call-update) | async-done | bytes 1572880 | tf_op jit(solution)/shard_map/all_gather | solution.py:178
  244.4 2.1 fusion.502
  246.6 1.6 fusion.17
  248.2 2.8 fusion.16
  251.0 2.8 convolution_add_fusion.1
  253.8 2.1 copy.373
  255.9 4.2 convolution_subtract_fusion.1
  260.1 2.1 copy.372
  264.8 1.7 multiply_bitcast_fusion.3
  267.3 10.6 %all_gather.14 = f32[3,64,1024]{2,1,0:T(8,128)S(1)} all-gather(f32[3,64,256]{2,1,0:T(8,128)S(1)} %pad_maximum_fusion.6), channel_id=1, replica_groups=mesh['strike'=64,'dip'=4] {'dip'}, dimensions={2}, use_global_device_ids=true | all-gather | bytes 983040 | tf_op jit(solution)/shard_map/all_gather | solution.py:158
  287.3 1.6 reshape.1796
  288.9 14.7 %all-to-all-start.2 = ((f32[64,1,1536]{2,1,0:T(1,128)}), f32[64,1,1536]{2,1,0:T(1,128)S(1)}, u32[]{:S(2)}, u32[]{:S(2)}) async-start(f32[64,1,1536]{2,1,0:T(1,128)} %reshape.1796), calls=%async_computation.2 | async-start | bytes 786432 | tf_op jit(solution)/shard_map/all_to_all | solution.py:172
  307.8 10.3 %all-to-all-done.2 = f32[64,1,1536]{2,1,0:T(1,128)S(1)} async-done(((f32[64,1,1536]{2,1,0:T(1,128)}), f32[64,1,1536]{2,1,0:T(1,128)S(1)}, u32[]{:S(2)}, u32[]{:S(2)}) %all-to-all-start.2) | async-done | bytes 393248 | tf_op jit(solution)/shard_map/all_to_all | solution.py:172
  318.1 1.6 reduce.2
  331.8 1.9 fusion.60
  336.6 10.3 %copy.396 = f32[3,1,4,4096]{2,1,0,3:T(1,128)} copy(f32[3,1,4,4096]{3,2,0,1:T(4,128)S(1)} %stack.193) | data formatting | bytes 393216 | tf_op jit(solution)/shard_map/stack | solution.py:155
  348.6 10.3 %copy.397 = f32[3,1,4,4096]{2,1,0,3:T(1,128)} copy(f32[3,1,4,4096]{3,2,0,1:T(4,128)S(1)} %stack.194) | data formatting | bytes 393216 | tf_op jit(solution)/shard_map/stack | solution.py:155
  358.8 16.7 %fusion.505 = f32[4096,3,2,4]{3,2,1,0:T(2,128)} fusion(f32[3,1,4,4096]{2,1,0,3:T(1,128)} %copy.397, f32[3,1,4,4096]{2,1,0,3:T(1,128)} %copy.396), kind=kLoop, calls=%fused_computation.663 | loop fusion | flops 98304 | bytes 786432
  375.5 16.7 %reshape.1798 = f32[64,1,1536]{2,1,0:T(1,128)S(1)} reshape(f32[4096,3,2,4]{3,2,1,0:T(2,128)} %fusion.505) | data formatting | bytes 786432
  392.3 20.6 %all_to_all.67 = f32[64,1,1536]{2,1,0:T(1,128)S(1)} all-to-all(f32[64,1,1536]{2,1,0:T(1,128)S(1)} %reshape.1798), channel_id=1, replica_groups=mesh['strike'=64,'dip'=4] {'strike'}, dimensions={0} | all-to-all | bytes 786432 | tf_op jit(solution)/shard_map/all_to_all | solution.py:177
  412.8 1.6 reduce.3
  414.4 21.1 %reshape.1799 = f32[4096,3,2,4]{3,2,1,0:T(2,128)} reshape(f32[64,1536]{1,0:T(8,128)S(1)} %reduce.3) | data formatting | bytes 786432
  435.5 15.9 %copy.467 = f32[3,2,4,64,64]{4,3,2,1,0:T(8,128)S(1)} copy(f32[3,2,4,64,64]{2,1,0,4,3:T(2,128)} %bitcast.477) | data formatting | bytes 786432 | tf_op jit(solution)/shard_map/all_to_all | solution.py:177
  451.5 1.4 copy.399
  452.9 37.3 %all-gather.5.cloned.1.call-done = f32[3,2,1024,64]{3,2,1,0:T(8,128)} async-done(((f32[3,2,256,64]{3,2,1,0:T(8,128)}), f32[3,2,1024,64]{3,2,1,0:T(8,128)}) %all-gather.5.cloned.1.call-update) | async-done | bytes 1572880 | tf_op jit(solution)/shard_map/all_gather | solution.py:178
  490.2 2.1 fusion.501
  492.4 1.6 fusion.19
  494.0 2.8 fusion.18
  496.8 2.8 convolution_add_fusion
  499.6 2.1 copy.403
  501.7 4.2 convolution_subtract_fusion
  505.9 2.1 copy.402
  510.6 1.8 multiply_add_fusion.17
  (191 shorter events, 78.3 us)
Async XLA Ops:
  28.9 16.8 %copy-start.34 = (s32[4,4096]{1,0:T(4,128)S(1)}, s32[4,4096]{1,0:T(4,128)}, u32[]{:S(2)}) copy-start(s32[4,4096]{1,0:T(4,128)} %param.9) | copy-start | bytes 196612
  28.9 16.8 %copy-start.33 = (bf16[4,3,2,4,4096]{4,3,2,1,0:T(4,128)(2,1)S(1)}, bf16[4,3,2,4,4096]{4,3,2,1,0:T(4,128)(2,1)}, u32[]{:S(2)}) copy-start(bf16[4,3,2,4,4096]{4,3,2,1,0:T(4,128)(2,1)} %param.8) | copy-start | bytes 2359300
  31.2 32.3 %all-to-all-start = ((f32[64,1,1536]{2,1,0:T(1,128)}), f32[64,1,1536]{2,1,0:T(1,128)S(1)}, u32[]{:S(2)}, u32[]{:S(2)}) async-start(f32[64,1,1536]{2,1,0:T(1,128)} %reshape.1792), calls=%async_computation | async-start | bytes 786432 | tf_op jit(solution)/shard_map/all_to_all | solution.py:172
  45.1 199.3 %all-gather.3.cloned.1.call-start = ((), (), s32[]{:S(2)}) async-start(), calls=%async_computation.4 | async-start | bytes 3932160 | tf_op jit(solution)/shard_map/all_gather | solution.py:178
  63.5 11.3 %copy-start.7 = (f32[4,64,64]{2,1,0:T(8,128)}, f32[4,64,64]{2,1,0:T(8,128)S(1)}, u32[]{:S(2)}) copy-start(f32[4,64,64]{2,1,0:T(8,128)S(1)} %get-tuple-element.73) | copy-start | bytes 196612
  63.5 12.3 %copy-start.1 = (f32[4,64,64]{2,1,0:T(8,128)}, f32[4,64,64]{2,1,0:T(8,128)S(1)}, u32[]{:S(2)}) copy-start(f32[4,64,64]{2,1,0:T(8,128)S(1)} %get-tuple-element.55) | copy-start | bytes 196612
  63.5 12.3 %copy-start.3 = (f32[4,64,64]{2,1,0:T(8,128)}, f32[4,64,64]{2,1,0:T(8,128)S(1)}, u32[]{:S(2)}) copy-start(f32[4,64,64]{2,1,0:T(8,128)S(1)} %get-tuple-element.56) | copy-start | bytes 196612
  63.5 12.3 %copy-start.5 = (f32[4,64,64]{2,1,0:T(8,128)}, f32[4,64,64]{2,1,0:T(8,128)S(1)}, u32[]{:S(2)}) copy-start(f32[4,64,64]{2,1,0:T(8,128)S(1)} %get-tuple-element.58) | copy-start | bytes 196612
  74.8 1.9 copy-start.18
  75.8 1.0 copy-start.10
  75.8 1.0 copy-start.11
  75.8 1.1 copy-start.12
  75.8 1.3 copy-start.13
  75.8 1.3 copy-start.14
  75.8 1.4 copy-start.15
  75.8 1.5 copy-start.16
  75.8 1.6 copy-start.17
  263.4 1.4 copy-start
  266.5 0.6 copy-start.25
  286.6 17.2 %copy-start.29 = (f32[1,2,4,4096]{3,2,1,0:T(4,128)S(1)}, f32[1,2,4,4096]{3,2,1,0:T(4,128)}, u32[]{:S(2)}) copy-start(f32[1,2,4,4096]{3,2,1,0:T(4,128)} %get-tuple-element.48) | copy-start | bytes 393220
  287.3 16.8 %copy-start.28 = (f32[1,2,4,4096]{3,2,1,0:T(4,128)S(1)}, f32[1,2,4,4096]{3,2,1,0:T(4,128)}, u32[]{:S(2)}) copy-start(f32[1,2,4,4096]{3,2,1,0:T(4,128)} %get-tuple-element.47) | copy-start | bytes 393220
  287.3 16.9 %copy-start.27 = (f32[1,2,4,4096]{3,2,1,0:T(4,128)S(1)}, f32[1,2,4,4096]{3,2,1,0:T(4,128)}, u32[]{:S(2)}) copy-start(f32[1,2,4,4096]{3,2,1,0:T(4,128)} %get-tuple-element.46) | copy-start | bytes 393220
  287.3 17.9 %copy-start.32 = (f32[1,2,4,4096]{3,2,1,0:T(4,128)S(1)}, f32[1,2,4,4096]{3,2,1,0:T(4,128)}, u32[]{:S(2)}) copy-start(f32[1,2,4,4096]{3,2,1,0:T(4,128)} %get-tuple-element.51) | copy-start | bytes 393220
  287.3 18.7 %copy-start.31 = (f32[1,2,4,4096]{3,2,1,0:T(4,128)S(1)}, f32[1,2,4,4096]{3,2,1,0:T(4,128)}, u32[]{:S(2)}) copy-start(f32[1,2,4,4096]{3,2,1,0:T(4,128)} %get-tuple-element.50) | copy-start | bytes 393220
  288.9 18.0 %copy-start.30 = (f32[1,2,4,4096]{3,2,1,0:T(4,128)S(1)}, f32[1,2,4,4096]{3,2,1,0:T(4,128)}, u32[]{:S(2)}) copy-start(f32[1,2,4,4096]{3,2,1,0:T(4,128)} %get-tuple-element.49) | copy-start | bytes 393220
  288.9 29.2 %all-to-all-start.2 = ((f32[64,1,1536]{2,1,0:T(1,128)}), f32[64,1,1536]{2,1,0:T(1,128)S(1)}, u32[]{:S(2)}, u32[]{:S(2)}) async-start(f32[64,1,1536]{2,1,0:T(1,128)} %reshape.1796), calls=%async_computation.2 | async-start | bytes 786432 | tf_op jit(solution)/shard_map/all_to_all | solution.py:172
  303.6 186.7 %all-gather.5.cloned.1.call-start = ((), (), s32[]{:S(2)}) async-start(), calls=%async_computation.5 | async-start | bytes 3932160 | tf_op jit(solution)/shard_map/all_gather | solution.py:178
  325.7 2.9 copy-start.2
  325.7 2.9 copy-start.4
  325.7 2.9 copy-start.6
  325.7 2.9 copy-start.8
  327.2 1.7 copy-start.9
  327.2 1.7 copy-start.19
  327.2 1.7 copy-start.20
  327.2 1.7 copy-start.21
  327.2 1.7 copy-start.22
  327.2 1.7 copy-start.23
  327.2 1.7 copy-start.24
  509.2 1.4 copy-start.26
Sparse Core Ops, SparseCore 0:
  205.5 38.8 all-gather.2
  453.0 37.1 all-gather.4
where the time goes:
time: 528 us; the launch traced here: 520 us
  local copies, waits for them, and re-layouts  189 us (36%)
  waiting for transfers between devices  86.6 us (16%)
  matrix products  75.4 us (14%)
  blocking collectives  69 us (13%)
  other arithmetic  56.3 us (11%)
  starting transfers between devices  29.3 us (6%)
  between operations  15.2 us (3%)
    unnamed x78, local copies, waits for them, and re-layouts  81.5 us
    all_gather x2, waiting for transfers between devices, to_space(): gathered = lax.all_gather(dip_spec, 'dip', axis=2, tiled=True)  76.3 us
    dot_general x56, matrix products, contract(): return jnp.einsum(pattern, first_operand, second_operand, precision=highest)  75.4 us
    all_to_all x2, blocking collectives, to_space(): lax.all_to_all(mixed_rows, 'strike', split_axis=3, concat_axis=2, tiled=T...  45.3 us
    another operation x8, local copies, waits for them, and re-layouts, strike_inverse(): jnp.stack([out_real, out_imag], axis=1)  42.1 us
    all_to_all x4, local copies, waits for them, and re-layouts, to_space(): lax.all_to_all(mixed_rows, 'strike', split_axis=3, concat_axis=2, tiled=T...  34.9 us
    unnamed x2, other arithmetic  33.4 us
    all_to_all x2, starting transfers between devices, to_modes(): lax.all_to_all(dip_spec, 'strike', split_axis=2, concat_axis=3, tiled=True)  28.6 us
  transfers between devices with their start and end apart: 4, of which 3 were waited for; matrix products, arithmetic and copies ran while one was open for 4% of the time, Pallas kernels for 0%

commit v1 on v0

--- a/solution.py
+++ b/solution.py
@@ -175,7 +175,20 @@
     def to_space(mode_field):
         mixed_rows = strike_inverse(mode_field)
         dip_spec = lax.all_to_all(mixed_rows, "strike", split_axis=3, concat_axis=2, tiled=True)
-        gathered = lax.all_gather(dip_spec, "dip", axis=2, tiled=True)
+
+        def unite_the_strings(device_axis, u_in):
+            vec_out = jnp.concatenate(
+                lax.all_to_all(
+                    jnp.stack(lax.psum(1, axis_name=device_axis) * [u_in]),
+                    concat_axis=0,
+                    axis_name=device_axis,
+                    split_axis=0,
+                ),
+                axis=2,
+            )
+            return vec_out
+
+        gathered = unite_the_strings("dip", dip_spec)
         grid_view = gathered.reshape(3, 2, dip_count, strike_count, mode_rows, row_count)
         cos_last, sin_last = phase_table(coarse_own, coarse_all, unit_modes)
         first_real, first_imag = pair_section(

time: 528 us -> 486 us (0.920)
  waiting for transfers between devices: 86.6 us -> 30.2 us
  blocking collectives: 69 us -> 92.9 us
  between operations: 15.2 us -> 1.92 us
    all_gather x2 -> x0, waiting for transfers between devices: 76.3 us -> none  [to_space(): gathered = lax.all_gather(dip_spec, 'dip', axis=2, tiled=True)]
    all_to_all x0 -> x1, blocking collectives: none -> 23 us  [unite_the_strings(): lax.all_to_all(jnp.stack(lax.psum(1, axis_name=device_axis) * [u_in]), co...]
    all_to_all x0 -> x1, waiting for transfers between devices: none -> 20 us  [unite_the_strings(): lax.all_to_all(jnp.stack(lax.psum(1, axis_name=device_axis) * [u_in]), co...]
  transfers between devices with their start and end apart: 4 -> 3, of which waited for: 3 -> 2; matrix products, arithmetic and copies ran while one was open for 4% -> 5% of each run, Pallas kernels for 0% -> 0%
where the time goes in v1:
time: 486 us; the launch traced here: 478 us
  local copies, waits for them, and re-layouts  192 us (40%)
  blocking collectives  92.9 us (19%)
  matrix products  75.1 us (15%)
  other arithmetic  56.3 us (12%)
  waiting for transfers between devices  30.2 us (6%)
  starting transfers between devices  29.5 us (6%)
    unnamed x78, local copies, waits for them, and re-layouts  81.4 us
    dot_general x56, matrix products, contract(): return jnp.einsum(pattern, first_operand, second_operand, precision=highest)  75.1 us
    all_to_all x2, blocking collectives, to_space(): lax.all_to_all(mixed_rows, 'strike', split_axis=3, concat_axis=2, tiled=T...  45.3 us
    another operation x8, local copies, waits for them, and re-layouts, strike_inverse(): jnp.stack([out_real, out_imag], axis=1)  42.1 us
    unnamed x2, other arithmetic  33.4 us
    all_to_all x4, local copies, waits for them, and re-layouts, to_space(): lax.all_to_all(mixed_rows, 'strike', split_axis=3, concat_axis=2, tiled=T...  32.5 us
    all_to_all x2, starting transfers between devices, to_modes(): lax.all_to_all(dip_spec, 'strike', split_axis=2, concat_axis=3, tiled=True)  24.9 us
    all_gather x2, blocking collectives, to_modes(): gathered = lax.all_gather(space_field, 'dip', axis=2, tiled=True)  24.7 us
  transfers between devices with their start and end apart: 3, of which 2 were waited for; matrix products, arithmetic and copies ran while one was open for 5% of the time, Pallas kernels for 0%

profile of v1, /device:TPU:1, one launch (start us, length us, event | category | flops | bytes accessed | tf_op | source)
XLA Modules:
  0.0 478.3 jit_solution(863347101783896501)
XLA Ops:
  0.8 13.1 %all_gather.6 = f32[3,64,1024]{2,1,0:T(8,128)S(1)} all-gather(f32[3,64,256]{2,1,0:T(8,128)} %param.7), channel_id=1, replica_groups=mesh['strike'=64,'dip'=4] {'dip'}, dimensions={2}, use_global_device_ids=true | all-gather | bytes 983040 | tf_op jit(solution)/shard_map/all_gather | solution.py:158
  23.0 1.6 reshape.1798
  24.6 14.4 %all-to-all-start = ((f32[64,1,1536]{2,1,0:T(1,128)}), f32[64,1,1536]{2,1,0:T(1,128)S(1)}, u32[]{:S(2)}, u32[]{:S(2)}) async-start(f32[64,1,1536]{2,1,0:T(1,128)} %reshape.1798), calls=%async_computation | async-start | bytes 786432 | tf_op jit(solution)/shard_map/all_to_all | solution.py:172
  39.3 4.1 multiply_add_fusion.20
  54.1 2.8 multiply_add_fusion.5
  77.9 10.6 %copy.378 = f32[3,1,4,4096]{2,1,0,3:T(1,128)} copy(f32[3,1,4,4096]{3,2,0,1:T(4,128)S(1)} %stack.189) | data formatting | bytes 393216 | tf_op jit(solution)/shard_map/stack | solution.py:155
  90.1 10.2 %copy.379 = f32[3,1,4,4096]{2,1,0,3:T(1,128)} copy(f32[3,1,4,4096]{3,2,0,1:T(4,128)S(1)} %stack.190) | data formatting | bytes 393216 | tf_op jit(solution)/shard_map/stack | solution.py:155
  100.3 16.7 %fusion.506 = f32[4096,3,2,4]{3,2,1,0:T(2,128)} fusion(f32[3,1,4,4096]{2,1,0,3:T(1,128)} %copy.379, f32[3,1,4,4096]{2,1,0,3:T(1,128)} %copy.378), kind=kLoop, calls=%fused_computation.664 | loop fusion | flops 98304 | bytes 786432
  117.0 16.7 %reshape.1800 = f32[64,1,1536]{2,1,0:T(1,128)S(1)} reshape(f32[4096,3,2,4]{3,2,1,0:T(2,128)} %fusion.506) | data formatting | bytes 786432
  133.8 24.7 %all_to_all.70 = f32[64,1,1536]{2,1,0:T(1,128)S(1)} all-to-all(f32[64,1,1536]{2,1,0:T(1,128)S(1)} %reshape.1800), channel_id=1, replica_groups=mesh['strike'=64,'dip'=4] {'strike'}, dimensions={0} | all-to-all | bytes 786432 | tf_op jit(solution)/shard_map/all_to_all | solution.py:177
  158.4 1.5 reduce.1
  160.0 21.1 %reshape.1801 = f32[4096,3,2,4]{3,2,1,0:T(2,128)} reshape(f32[64,1536]{1,0:T(8,128)S(1)} %reduce.1) | data formatting | bytes 786432
  181.1 15.7 %copy.471 = f32[3,2,4,64,64]{4,3,2,1,0:T(8,128)S(1)} copy(f32[3,2,4,64,64]{2,1,0,4,3:T(2,128)} %bitcast.480) | data formatting | bytes 786432 | tf_op jit(solution)/shard_map/all_to_all | solution.py:177
  199.0 4.6 all-to-all-start.2
  203.6 20.0 %all-to-all-done.2 = f32[4,3,2,256,64]{3,4,2,1,0:T(8,128)S(1)} async-done(((f32[4,3,2,256,64]{3,4,2,1,0:T(8,128)}), f32[4,3,2,256,64]{3,4,2,1,0:T(8,128)S(1)}, u32[]{:S(2)}, u32[]{:S(2)}) %all-to-all-start.2) | async-done | bytes 1572896 | tf_op jit(solution)/shard_map/all_to_all | solution.py:181
  223.6 2.2 copy.383
  225.9 2.1 fusion.502
  228.0 1.6 fusion.17
  229.7 2.8 fusion.16
  232.4 2.8 convolution_add_fusion.1
  235.2 2.1 copy.387
  237.4 4.2 convolution_subtract_fusion.1
  241.6 2.1 copy.386
  246.2 1.7 multiply_bitcast_fusion.3
  248.8 11.6 %all_gather.7 = f32[3,64,1024]{2,1,0:T(8,128)S(1)} all-gather(f32[3,64,256]{2,1,0:T(8,128)S(1)} %pad_maximum_fusion.6), channel_id=1, replica_groups=mesh['strike'=64,'dip'=4] {'dip'}, dimensions={2}, use_global_device_ids=true | all-gather | bytes 983040 | tf_op jit(solution)/shard_map/all_gather | solution.py:158
  269.7 1.6 reshape.1802
  271.3 10.6 %all-to-all-start.3 = ((f32[64,1,1536]{2,1,0:T(1,128)}), f32[64,1,1536]{2,1,0:T(1,128)S(1)}, u32[]{:S(2)}, u32[]{:S(2)}) async-start(f32[64,1,1536]{2,1,0:T(1,128)} %reshape.1802), calls=%async_computation.3 | async-start | bytes 786432 | tf_op jit(solution)/shard_map/all_to_all | solution.py:172
  285.9 10.1 %all-to-all-done.3 = f32[64,1,1536]{2,1,0:T(1,128)S(1)} async-done(((f32[64,1,1536]{2,1,0:T(1,128)}), f32[64,1,1536]{2,1,0:T(1,128)S(1)}, u32[]{:S(2)}, u32[]{:S(2)}) %all-to-all-start.3) | async-done | bytes 393248 | tf_op jit(solution)/shard_map/all_to_all | solution.py:172
  296.0 1.5 reduce.2
  309.6 1.6 fusion.60
  314.2 10.4 %copy.410 = f32[3,1,4,4096]{2,1,0,3:T(1,128)} copy(f32[3,1,4,4096]{3,2,0,1:T(4,128)S(1)} %stack.213) | data formatting | bytes 393216 | tf_op jit(solution)/shard_map/stack | solution.py:155
  326.1 10.2 %copy.411 = f32[3,1,4,4096]{2,1,0,3:T(1,128)} copy(f32[3,1,4,4096]{3,2,0,1:T(4,128)S(1)} %stack.214) | data formatting | bytes 393216 | tf_op jit(solution)/shard_map/stack | solution.py:155
  336.4 16.7 %fusion.505 = f32[4096,3,2,4]{3,2,1,0:T(2,128)} fusion(f32[3,1,4,4096]{2,1,0,3:T(1,128)} %copy.411, f32[3,1,4,4096]{2,1,0,3:T(1,128)} %copy.410), kind=kLoop, calls=%fused_computation.663 | loop fusion | flops 98304 | bytes 786432
  353.1 16.7 %reshape.1804 = f32[64,1,1536]{2,1,0:T(1,128)S(1)} reshape(f32[4096,3,2,4]{3,2,1,0:T(2,128)} %fusion.505) | data formatting | bytes 786432
  369.8 20.6 %all_to_all.71 = f32[64,1,1536]{2,1,0:T(1,128)S(1)} all-to-all(f32[64,1,1536]{2,1,0:T(1,128)S(1)} %reshape.1804), channel_id=1, replica_groups=mesh['strike'=64,'dip'=4] {'strike'}, dimensions={0} | all-to-all | bytes 786432 | tf_op jit(solution)/shard_map/all_to_all | solution.py:177
  390.4 1.5 reduce.3
  392.0 21.1 %reshape.1805 = f32[4096,3,2,4]{3,2,1,0:T(2,128)} reshape(f32[64,1536]{1,0:T(8,128)S(1)} %reduce.3) | data formatting | bytes 786432
  413.1 15.7 %copy.483 = f32[3,2,4,64,64]{4,3,2,1,0:T(8,128)S(1)} copy(f32[3,2,4,64,64]{2,1,0,4,3:T(2,128)} %bitcast.481) | data formatting | bytes 786432 | tf_op jit(solution)/shard_map/all_to_all | solution.py:177
  429.8 23.0 %all_to_all.72 = f32[4,3,2,256,64]{3,4,2,1,0:T(8,128)S(1)} all-to-all(f32[4,3,2,256,64]{3,4,2,1,0:T(8,128)S(1)} %stack.217), channel_id=1, replica_groups=mesh['strike'=64,'dip'=4] {'dip'}, dimensions={0} | all-to-all | bytes 3145728 | tf_op jit(solution)/shard_map/all_to_all | solution.py:181
  452.8 2.2 copy.415
  455.0 2.1 fusion.501
  457.2 1.6 fusion.19
  458.8 2.8 fusion.18
  461.6 2.8 convolution_add_fusion
  464.4 2.1 copy.419
  466.5 4.2 convolution_subtract_fusion
  470.7 2.1 copy.418
  475.4 1.8 multiply_add_fusion.17
  (194 shorter events, 82.0 us)
Async XLA Ops:
  22.4 16.7 %copy-start.34 = (s32[4,4096]{1,0:T(4,128)S(1)}, s32[4,4096]{1,0:T(4,128)}, u32[]{:S(2)}) copy-start(s32[4,4096]{1,0:T(4,128)} %param.9) | copy-start | bytes 196612
  22.4 16.8 %copy-start.33 = (bf16[4,3,2,4,4096]{4,3,2,1,0:T(4,128)(2,1)S(1)}, bf16[4,3,2,4,4096]{4,3,2,1,0:T(4,128)(2,1)}, u32[]{:S(2)}) copy-start(bf16[4,3,2,4,4096]{4,3,2,1,0:T(4,128)(2,1)} %param.8) | copy-start | bytes 2359300
  24.6 32.3 %all-to-all-start = ((f32[64,1,1536]{2,1,0:T(1,128)}), f32[64,1,1536]{2,1,0:T(1,128)S(1)}, u32[]{:S(2)}, u32[]{:S(2)}) async-start(f32[64,1,1536]{2,1,0:T(1,128)} %reshape.1798), calls=%async_computation | async-start | bytes 786432 | tf_op jit(solution)/shard_map/all_to_all | solution.py:172
  56.9 11.2 %copy-start.7 = (f32[4,64,64]{2,1,0:T(8,128)}, f32[4,64,64]{2,1,0:T(8,128)S(1)}, u32[]{:S(2)}) copy-start(f32[4,64,64]{2,1,0:T(8,128)S(1)} %get-tuple-element.73) | copy-start | bytes 196612
  56.9 12.3 %copy-start.1 = (f32[4,64,64]{2,1,0:T(8,128)}, f32[4,64,64]{2,1,0:T(8,128)S(1)}, u32[]{:S(2)}) copy-start(f32[4,64,64]{2,1,0:T(8,128)S(1)} %get-tuple-element.55) | copy-start | bytes 196612
  56.9 12.3 %copy-start.3 = (f32[4,64,64]{2,1,0:T(8,128)}, f32[4,64,64]{2,1,0:T(8,128)S(1)}, u32[]{:S(2)}) copy-start(f32[4,64,64]{2,1,0:T(8,128)S(1)} %get-tuple-element.56) | copy-start | bytes 196612
  56.9 12.3 %copy-start.5 = (f32[4,64,64]{2,1,0:T(8,128)}, f32[4,64,64]{2,1,0:T(8,128)S(1)}, u32[]{:S(2)}) copy-start(f32[4,64,64]{2,1,0:T(8,128)S(1)} %get-tuple-element.58) | copy-start | bytes 196612
  68.1 1.9 copy-start.18
  69.1 1.0 copy-start.10
  69.1 1.0 copy-start.11
  69.1 1.1 copy-start.12
  69.1 1.3 copy-start.13
  69.1 1.3 copy-start.14
  69.1 1.4 copy-start.15
  69.1 1.5 copy-start.16
  69.1 1.6 copy-start.17
  199.0 24.7 %all-to-all-start.2 = ((f32[4,3,2,256,64]{3,4,2,1,0:T(8,128)}), f32[4,3,2,256,64]{3,4,2,1,0:T(8,128)S(1)}, u32[]{:S(2)}, u32[]{:S(2)}) async-start(f32[4,3,2,256,64]{3,4,2,1,0:T(8,128)} %stack.193), calls=%async_computation.2 | async-start | bytes 3145728 | tf_op jit(solution)/shard_map/all_to_all | solution.py:181
  244.8 1.4 copy-start
  247.9 0.6 copy-start.25
  269.0 12.8 %copy-start.29 = (f32[1,2,4,4096]{3,2,1,0:T(4,128)S(1)}, f32[1,2,4,4096]{3,2,1,0:T(4,128)}, u32[]{:S(2)}) copy-start(f32[1,2,4,4096]{3,2,1,0:T(4,128)} %get-tuple-element.48) | copy-start | bytes 393220
  269.6 12.4 %copy-start.28 = (f32[1,2,4,4096]{3,2,1,0:T(4,128)S(1)}, f32[1,2,4,4096]{3,2,1,0:T(4,128)}, u32[]{:S(2)}) copy-start(f32[1,2,4,4096]{3,2,1,0:T(4,128)} %get-tuple-element.47) | copy-start | bytes 393220
  269.7 12.6 %copy-start.27 = (f32[1,2,4,4096]{3,2,1,0:T(4,128)S(1)}, f32[1,2,4,4096]{3,2,1,0:T(4,128)}, u32[]{:S(2)}) copy-start(f32[1,2,4,4096]{3,2,1,0:T(4,128)} %get-tuple-element.46) | copy-start | bytes 393220
  269.7 13.5 %copy-start.32 = (f32[1,2,4,4096]{3,2,1,0:T(4,128)S(1)}, f32[1,2,4,4096]{3,2,1,0:T(4,128)}, u32[]{:S(2)}) copy-start(f32[1,2,4,4096]{3,2,1,0:T(4,128)} %get-tuple-element.51) | copy-start | bytes 393220
  269.7 14.4 %copy-start.31 = (f32[1,2,4,4096]{3,2,1,0:T(4,128)S(1)}, f32[1,2,4,4096]{3,2,1,0:T(4,128)}, u32[]{:S(2)}) copy-start(f32[1,2,4,4096]{3,2,1,0:T(4,128)} %get-tuple-element.50) | copy-start | bytes 393220
  271.3 13.7 %copy-start.30 = (f32[1,2,4,4096]{3,2,1,0:T(4,128)S(1)}, f32[1,2,4,4096]{3,2,1,0:T(4,128)}, u32[]{:S(2)}) copy-start(f32[1,2,4,4096]{3,2,1,0:T(4,128)} %get-tuple-element.49) | copy-start | bytes 393220
  271.3 24.7 %all-to-all-start.3 = ((f32[64,1,1536]{2,1,0:T(1,128)}), f32[64,1,1536]{2,1,0:T(1,128)S(1)}, u32[]{:S(2)}, u32[]{:S(2)}) async-start(f32[64,1,1536]{2,1,0:T(1,128)} %reshape.1802), calls=%async_computation.3 | async-start | bytes 786432 | tf_op jit(solution)/shard_map/all_to_all | solution.py:172
  303.6 2.9 copy-start.2
  303.6 2.9 copy-start.4
  303.6 2.9 copy-start.6
  303.6 2.9 copy-start.8
  305.0 1.7 copy-start.9
  305.0 1.7 copy-start.19
  305.0 1.7 copy-start.20
  305.0 1.7 copy-start.21
  305.1 1.7 copy-start.22
  305.1 1.7 copy-start.23
  305.1 1.7 copy-start.24
  473.9 1.4 copy-start.26
